TPU v7x, 32 devices: a whole 2x2x4 slice. The times are simulated.
32 devices in a mesh: dp: 4 (over y, x), expert: 8 (over z, core).
Axes of the slice: x: 2, y: 2, z: 4, core: 2. Of those that a mesh axis runs over, the one named last changes fastest.
Arguments:
- tokens: bfloat16 [5120, 1024], P(('dp', 'expert')), may hold values from -6 to 6
- expert_ids: int32 [5120, 2], P(('dp', 'expert')), may hold values from 0 to 15, all different within a row; in each aligned block of 160 rows (0 to 159, 160 to 319, ...) at most 40 rows name the same one
- router: bfloat16 [1024, 16], replicated, may hold values from -0.5 to 0.5
- gate_up_weight: bfloat16 [16, 1024, 2048], P('expert', 'dp'), may hold values from -0.1875 to 0.1875
- down_weight: bfloat16 [16, 1024, 1024], P('expert', 'dp'), may hold values from -0.1875 to 0.1875
- out_grad: bfloat16 [5120, 1024], P(('dp', 'expert')), may hold values from -6 to 6
Outputs:
- mixed_out: bfloat16 [5120, 1024], P(('dp', 'expert'))
- tokens_grad: bfloat16 [5120, 1024], P(('dp', 'expert'))
- router_grad: float32 [1024, 16], replicated
- gate_up_grad: float32 [16, 1024, 2048], P('expert', 'dp')
- down_grad: float32 [16, 1024, 1024], P('expert', 'dp')
Inputs may be any that keep to these rules, and one draw needn't show every extreme that they name: `expert_ids`: the 2 experts of a token differ. Among the 160 tokens of one device no expert is named more than 40 times, and in every draw some expert is named exactly 40 times by the tokens of some device.
All inputs are finite; a program needn't handle non-finite values.
Results may differ from a plain program's by a relative error of at most 0.013.
Values may be sent and summed in bfloat16 or wider, within the bound.
A program may use at most 128 MiB of HBM per device.

v0:
```python
import jax
import jax.numpy as jnp
from jax import lax
from jax.sharding import PartitionSpec as P


def activate(gate_up, hidden_units):
    gate_part = gate_up[..., :hidden_units]
    up_part = gate_up[..., hidden_units:]
    sigmoid_gate = jax.nn.sigmoid(gate_part)
    active = gate_part * sigmoid_gate
    return ((active * up_part).astype(jnp.bfloat16), gate_part, up_part, sigmoid_gate, active)


def finish_rows(gate_up, full_down):
    hidden = activate(gate_up, full_down.shape[1])[0]
    produced = jnp.einsum(
        "sjcf,jfd->sjcd", hidden, full_down, preferred_element_type=jnp.float32
    ).astype(jnp.bfloat16)
    return lax.all_to_all(produced, "expert", split_axis=0, concat_axis=0, tiled=True)


def on_device(tokens, expert_ids, router, gate_up_weight, down_weight, out_grad):
    full_gate_up, full_down = (
        lax.all_gather(gate_up_weight, "dp", axis=1, tiled=True),
        lax.all_gather(down_weight, "dp", axis=1, tiled=True),
    )
    token_rows = tokens.shape[0]
    feature_dim = tokens.shape[1]
    pair_count = expert_ids.shape[1]
    owners = lax.axis_size("expert")
    local_count = full_gate_up.shape[0]
    experts = owners * local_count
    capacity = 2 * pair_count * token_rows // experts
    hidden_units = full_down.shape[1]
    slot_total = experts * capacity
    onehot = (expert_ids[:, :, None] == jnp.arange(experts, dtype=jnp.int32)[None, None, :]).astype(
        jnp.int32
    )
    per_token = jnp.sum(onehot, axis=1)
    before = jnp.cumsum(per_token, axis=0) - per_token
    position = jnp.sum(before[:, None, :] * onehot, axis=2)
    slot_index = expert_ids * capacity + position
    select = (
        slot_index[:, :, None] == jnp.arange(slot_total, dtype=jnp.int32)[None, None, :]
    ).astype(jnp.bfloat16)
    dispatch = select[:, 0, :] + select[:, 1, :]
    send_rows = jnp.dot(dispatch.T, tokens, preferred_element_type=jnp.float32).astype(jnp.bfloat16)
    send_rows = send_rows.reshape(owners, local_count, capacity, feature_dim)
    logits = jnp.dot(tokens, router, preferred_element_type=jnp.float32)
    onehot_float = onehot.astype(jnp.float32)
    chosen = jnp.sum(logits[:, None, :] * onehot_float, axis=2)
    gate_first = jax.nn.sigmoid(chosen[:, 0] - chosen[:, 1])
    gate_pair = jnp.stack([gate_first, 1.0 - gate_first], axis=1)
    received = lax.all_to_all(send_rows, "expert", split_axis=0, concat_axis=0, tiled=True)
    gate_up = jnp.einsum(
        "sjcd,jdf->sjcf", received, full_gate_up, preferred_element_type=jnp.float32
    )
    returned = finish_rows(gate_up, full_down)
    returned_flat = returned.reshape(slot_total, feature_dim)
    expert_out = jnp.einsum(
        "tks,sd->tkd", select, returned_flat, preferred_element_type=jnp.float32
    )
    mixed_out = jnp.sum(gate_pair[:, :, None] * expert_out, axis=1).astype(jnp.bfloat16)
    grad_float = out_grad.astype(jnp.float32)
    gate_grads = jnp.sum(grad_float[:, None, :] * expert_out, axis=2)
    common = gate_pair[:, 0] * gate_pair[:, 1] * (gate_grads[:, 0] - gate_grads[:, 1])
    logit_grads = common[:, None] * (onehot_float[:, 0, :] - onehot_float[:, 1, :])
    scaled = (gate_pair[:, :, None] * grad_float[:, None, :]).astype(jnp.bfloat16)
    grad_send = jnp.einsum(
        "tks,tkd->sd", select, scaled, preferred_element_type=jnp.float32
    ).astype(jnp.bfloat16)
    grad_send = grad_send.reshape(owners, local_count, capacity, feature_dim)
    grad_recv = lax.all_to_all(grad_send, "expert", split_axis=0, concat_axis=0, tiled=True)
    hidden, gate_part, up_part, sigmoid_gate, active = activate(gate_up, hidden_units)
    hidden_grad = jnp.einsum(
        "sjcd,jfd->sjcf", grad_recv, full_down, preferred_element_type=jnp.float32
    )
    gate_grad = hidden_grad * up_part * sigmoid_gate * (1.0 + gate_part * (1.0 - sigmoid_gate))
    up_grad = hidden_grad * active
    pre_grad = jnp.concatenate([gate_grad, up_grad], axis=3).astype(jnp.bfloat16)
    input_grad = jnp.einsum(
        "sjcf,jdf->sjcd", pre_grad, full_gate_up, preferred_element_type=jnp.float32
    ).astype(jnp.bfloat16)
    input_back = lax.all_to_all(input_grad, "expert", split_axis=0, concat_axis=0, tiled=True)
    input_pair = jnp.einsum(
        "tks,sd->td",
        select,
        input_back.reshape(slot_total, feature_dim),
        preferred_element_type=jnp.float32,
    )
    router_float = router.astype(jnp.float32)
    tokens_grad = (
        input_pair + jnp.dot(logit_grads, router_float.T, precision=lax.Precision.HIGHEST)
    ).astype(jnp.bfloat16)
    router_term = jnp.dot(
        tokens.astype(jnp.float32).T, logit_grads, precision=lax.Precision.HIGHEST
    )
    router_grad = lax.psum(router_term, ("dp", "expert"))
    gate_up_part = jnp.einsum(
        "sjcd,sjcf->jdf", received, pre_grad, preferred_element_type=jnp.float32
    )
    down_part = jnp.einsum("sjcf,sjcd->jfd", hidden, grad_recv, preferred_element_type=jnp.float32)
    gate_up_grad, down_grad = (
        lax.psum_scatter(
            gate_up_part.astype(jnp.bfloat16), "dp", scatter_dimension=1, tiled=True
        ).astype(jnp.float32),
        lax.psum_scatter(
            down_part.astype(jnp.bfloat16), "dp", scatter_dimension=1, tiled=True
        ).astype(jnp.float32),
    )
    return (mixed_out, tokens_grad, router_grad, gate_up_grad, down_grad)


def solution(mesh):
    placed = (
        P(("dp", "expert"), None),
        P(("dp", "expert"), None),
        P(),
        P("expert", "dp", None),
        P("expert", "dp", None),
        P(("dp", "expert"), None),
    )
    return jax.shard_map(
        on_device,
        mesh=mesh,
        in_specs=placed,
        out_specs=(
            P(("dp", "expert"), None),
            P(("dp", "expert"), None),
            P(),
            P("expert", "dp", None),
            P("expert", "dp", None),
        ),
        check_vma=False,
    )
```

profile of v0, /device:TPU:1, one launch (start us, length us, event | category | flops | bytes accessed | tf_op | source)
XLA Modules:
  0.0 444.5 jit_solution(6109489005997214316)
XLA Ops:
  7.2 0.7 all-gather.3.cloned.1.call-update
  8.0 0.7 all-gather.5.cloned.1.call-update
  9.8 1.6 convolution_convert_fusion
  11.4 6.5 %all-to-all-start = ((bf16[8,2,40,1024]{3,2,1,0:T(8,128)(2,1)}), bf16[8,2,40,1024]{3,2,1,0:T(8,128)(2,1)S(1)}, u32[]{:S(2)}, u32[]{:S(2)}) async-start(bf16[8,2,40,1024]{3,2,1,0:T(8,128)(2,1)} %bitcast.3), calls=%async_computation | async-start | bytes 2621440 | tf_op jit(solution)/shard_map/all_to_all | solution.py:55
  18.8 2.0 bitcast_convert_fusion.2
  20.8 28.3 %all-to-all-done = bf16[8,2,40,1024]{3,2,1,0:T(8,128)(2,1)S(1)} async-done(((bf16[8,2,40,1024]{3,2,1,0:T(8,128)(2,1)}), bf16[8,2,40,1024]{3,2,1,0:T(8,128)(2,1)S(1)}, u32[]{:S(2)}, u32[]{:S(2)}) %all-to-all-start) | async-done | bytes 1310752 | tf_op jit(solution)/shard_map/all_to_all | solution.py:55
  49.1 4.4 all-to-all-start.2
  53.6 45.8 %all-gather.3.cloned.1.call-done = bf16[2,1024,2048]{2,1,0:T(8,128)(2,1)} async-done(((bf16[2,256,2048]{2,1,0:T(8,128)(2,1)}), bf16[2,1024,2048]{2,1,0:T(8,128)(2,1)}) %all-gather.3.cloned.1.call-update) | async-done | bytes 8388624 | tf_op jit(solution)/shard_map/all_gather | solution.py:25
  99.3 8.1 %fusion.8 = f32[8,2,40,2048]{3,2,0,1:T(8,128)} fusion(bf16[2,1024,2048]{2,1,0:T(8,128)(2,1)} %all-gather.3.cloned.1.call-done, bf16[8,2,40,1024]{3,2,1,0:T(8,128)(2,1)S(1)} %all-to-all-done), kind=kOutput, calls=%fused_computation.10 | convolution fusion | flops 2684354560 | bytes 14942208 | tf_op jit(solution)/shard_map/sjcd,jdf->sjcf/dot_general | solution.py:56
  107.4 46.4 %all-gather.5.cloned.1.call-done = bf16[2,1024,1024]{2,1,0:T(8,128)(2,1)} async-done(((bf16[2,256,1024]{2,1,0:T(8,128)(2,1)}), bf16[2,1024,1024]{2,1,0:T(8,128)(2,1)}) %all-gather.5.cloned.1.call-update) | async-done | bytes 4194320 | tf_op jit(solution)/shard_map/all_gather | solution.py:26
  153.8 7.7 %fusion.13 = (bf16[8,2,40,1024]{3,2,0,1:T(8,128)(2,1)}, bf16[8,2,40,1024]{3,2,0,1:T(8,128)(2,1)}, bf16[8,2,40,1024]{3,2,0,1:T(8,128)(2,1)S(1)}) fusion(f32[8,2,40,2048]{3,2,0,1:T(8,128)} %fusion.8, bf16[2,1024,1024]{2,1,0:T(8,128)(2,1)} %all-gather.5.cloned.1.call-done, bf16[8,2,40,1024]{3,2,1,0:T(8,128)(2,1)S(1)} %all-to-all-done.2), kind=kOutput, calls=%fused_computation.16 | convolution fusion | flops 1352007680 | bytes 14680064 | tf_op jit(solution)/shard_map/sjcd,jfd->sjcf/dot_general | solution.py:76
  161.5 1.2 copy-done.7
  162.7 4.4 bitcast_convert_fusion.1
  167.1 1.2 copy-done.5
  168.4 8.1 %bitcast_convert_fusion = bf16[2,1024,2048]{2,1,0:T(8,128)(2,1)} fusion(bf16[8,2,40,1024]{3,2,1,0:T(8,128)(2,1)S(1)} %all-to-all-done, bf16[8,2,40,1024]{3,2,0,1:T(8,128)(2,1)} %get-tuple-element.10, bf16[8,2,40,1024]{3,2,0,1:T(8,128)(2,1)S(1)} %copy-done.5), kind=kOutput, calls=%fused_computation | convolution fusion | flops 2693791744 | bytes 12320768 | tf_op jit(solution)/shard_map/sjcd,sjcf->jdf/dot_general | solution.py:100
  176.5 1.3 copy-done.8
  177.8 3.7 fusion.26
  181.5 1.2 copy.38
  182.7 5.6 %all-to-all-start.1 = ((bf16[8,2,40,1024]{3,2,1,0:T(8,128)(2,1)}), bf16[8,2,40,1024]{3,2,1,0:T(8,128)(2,1)S(1)}, u32[]{:S(2)}, u32[]{:S(2)}) async-start(bf16[8,2,40,1024]{3,2,1,0:T(8,128)(2,1)} %copy.38), calls=%async_computation.1 | async-start | bytes 2621440 | tf_op jit(solution)/shard_map/all_to_all | solution.py:20
  188.2 6.9 %fusion.23 = bf16[8,2,40,1024]{3,2,0,1:T(8,128)(2,1)S(1)} fusion(bf16[2,1024,2048]{2,1,0:T(8,128)(2,1)} %all-gather.3.cloned.1.call-done, bf16[8,2,40,1024]{3,2,0,1:T(8,128)(2,1)} %get-tuple-element.10, bf16[8,2,40,1024]{3,2,0,1:T(8,128)(2,1)S(1)} %copy-done.6), kind=kOutput, calls=%fused_computation.26 | convolution fusion | flops 2690252800 | bytes 12320768 | tf_op jit(solution)/shard_map/sjcf,jdf->sjcd/dot_general | solution.py:82
  195.1 1.2 copy.40
  196.3 23.2 %all-to-all-done.1 = bf16[8,2,40,1024]{3,2,1,0:T(8,128)(2,1)S(1)} async-done(((bf16[8,2,40,1024]{3,2,1,0:T(8,128)(2,1)}), bf16[8,2,40,1024]{3,2,1,0:T(8,128)(2,1)S(1)}, u32[]{:S(2)}, u32[]{:S(2)}) %all-to-all-start.1) | async-done | bytes 1310752 | tf_op jit(solution)/shard_map/all_to_all | solution.py:20
  219.4 4.4 all-to-all-start.3
  224.1 2.8 multiply_reduce_fusion
  226.8 0.9 convolution_bitcast_fusion
  227.7 27.4 %all-to-all-done.3 = bf16[8,2,40,1024]{3,2,1,0:T(8,128)(2,1)S(1)} async-done(((bf16[8,2,40,1024]{3,2,1,0:T(8,128)(2,1)}), bf16[8,2,40,1024]{3,2,1,0:T(8,128)(2,1)S(1)}, u32[]{:S(2)}, u32[]{:S(2)}) %all-to-all-start.3) | async-done | bytes 1310752 | tf_op jit(solution)/shard_map/all_to_all | solution.py:85
  255.6 1.2 fusion.30
  256.8 2.8 convert_element_type.79
  259.6 49.5 %reduce-scatter.3.cloned.1.call-done = bf16[2,256,2048]{2,1,0:T(8,128)(2,1)} async-done(((bf16[2,1024,2048]{2,1,0:T(8,128)(2,1)}), bf16[2,256,2048]{2,1,0:T(8,128)(2,1)}) %reduce-scatter.3.cloned.1.call-update) | async-done | bytes 2097168 | tf_op jit(solution)/shard_map/reduce_scatter | solution.py:105
  309.1 4.1 convert_element_type.77
  313.2 123.3 %all-reduce.3.cloned.1.call-done = f32[1024,16]{0,1:T(8,128)} async-done(((f32[1024,16]{0,1:T(8,128)}), f32[1024,16]{0,1:T(8,128)}) %all-reduce.3.cloned.1.call-update) | async-done | bytes 65552 | tf_op jit(solution)/shard_map/psum | solution.py:99
  436.5 1.5 copy.61
  (45 shorter events, 2.7 us)
Async XLA Ops:
  7.2 2.6 copy-start
  7.2 1.5 copy-start.4
  7.2 92.2 %all-gather.3.cloned.1.call-start = ((), (), s32[]{:S(2)}) async-start(), calls=%async_computation.6 | async-start | bytes 10485760 | tf_op jit(solution)/shard_map/all_gather | solution.py:25
  7.9 145.9 %all-gather.5.cloned.1.call-start = ((), (), s32[]{:S(2)}) async-start(), calls=%async_computation.7 | async-start | bytes 5242880 | tf_op jit(solution)/shard_map/all_gather | solution.py:26
  11.4 6.5 %copy-start.2 = (bf16[160,1024]{1,0:T(8,128)(2,1)S(1)}, bf16[160,1024]{1,0:T(8,128)(2,1)}, u32[]{:S(2)}) copy-start(bf16[160,1024]{1,0:T(8,128)(2,1)} %param.11) | copy-start | bytes 983044
  11.4 6.6 %copy-start.3 = (bf16[1024,16]{0,1:T(8,128)(2,1)S(1)}, bf16[1024,16]{0,1:T(8,128)(2,1)}, u32[]{:S(2)}) copy-start(bf16[1024,16]{0,1:T(8,128)(2,1)} %param.8) | copy-start | bytes 98308
  11.4 37.7 %all-to-all-start = ((bf16[8,2,40,1024]{3,2,1,0:T(8,128)(2,1)}), bf16[8,2,40,1024]{3,2,1,0:T(8,128)(2,1)S(1)}, u32[]{:S(2)}, u32[]{:S(2)}) async-start(bf16[8,2,40,1024]{3,2,1,0:T(8,128)(2,1)} %bitcast.3), calls=%async_computation | async-start | bytes 2621440 | tf_op jit(solution)/shard_map/all_to_all | solution.py:55
  18.0 0.8 copy-start.1
  49.1 58.3 %all-to-all-start.2 = ((bf16[8,2,40,1024]{3,2,1,0:T(8,128)(2,1)}), bf16[8,2,40,1024]{3,2,1,0:T(8,128)(2,1)S(1)}, u32[]{:S(2)}, u32[]{:S(2)}) async-start(bf16[8,2,40,1024]{3,2,1,0:T(8,128)(2,1)} %bitcast.94), calls=%async_computation.2 | async-start | bytes 2621440 | tf_op jit(solution)/shard_map/all_to_all | solution.py:74
  53.6 203.2 %reduce-scatter.5.cloned.1.call-start = ((), (), s32[]{:S(2)}) async-start(), calls=%async_computation.10 | async-start | bytes 5242880 | tf_op jit(solution)/shard_map/reduce_scatter | solution.py:108
  161.5 1.2 copy-start.7
  167.1 1.3 copy-start.5
  167.1 142.0 %reduce-scatter.3.cloned.1.call-start = ((), (), s32[]{:S(2)}) async-start(), calls=%async_computation.9 | async-start | bytes 10485760 | tf_op jit(solution)/shard_map/reduce_scatter | solution.py:105
  176.5 1.3 copy-start.8
  182.7 5.6 %copy-start.6 = (bf16[8,2,40,1024]{3,2,0,1:T(8,128)(2,1)S(1)}, bf16[8,2,40,1024]{3,2,0,1:T(8,128)(2,1)}, u32[]{:S(2)}) copy-start(bf16[8,2,40,1024]{3,2,0,1:T(8,128)(2,1)} %get-tuple-element.9) | copy-start | bytes 3932164
  182.7 36.8 %all-to-all-start.1 = ((bf16[8,2,40,1024]{3,2,1,0:T(8,128)(2,1)}), bf16[8,2,40,1024]{3,2,1,0:T(8,128)(2,1)S(1)}, u32[]{:S(2)}, u32[]{:S(2)}) async-start(bf16[8,2,40,1024]{3,2,1,0:T(8,128)(2,1)} %copy.38), calls=%async_computation.1 | async-start | bytes 2621440 | tf_op jit(solution)/shard_map/all_to_all | solution.py:20
  219.4 35.7 %all-to-all-start.3 = ((bf16[8,2,40,1024]{3,2,1,0:T(8,128)(2,1)}), bf16[8,2,40,1024]{3,2,1,0:T(8,128)(2,1)S(1)}, u32[]{:S(2)}, u32[]{:S(2)}) async-start(bf16[8,2,40,1024]{3,2,1,0:T(8,128)(2,1)} %copy.40), calls=%async_computation.3 | async-start | bytes 2621440 | tf_op jit(solution)/shard_map/all_to_all | solution.py:85
  223.9 212.7 %all-reduce.3.cloned.1.call-start = ((), (), s32[]{:S(2)}) async-start(), calls=%async_computation.8 | async-start | bytes 131072 | tf_op jit(solution)/shard_map/psum | solution.py:99
Sparse Core Ops, SparseCore 0:
  9.8 89.4 all-gather.2
  101.2 52.5 all-gather.4
  167.2 52.5 reduce-scatter.4
  222.7 86.3 reduce-scatter.2
  315.1 121.4 all-reduce.2
where the time goes:
time: 445 us
  waiting for transfers between devices  345 us (78%)
  matrix products  47.9 us (11%)
  starting transfers between devices  21.1 us (5%)
  between operations  13.9 us (3%)
  local copies, waits for them, and re-layouts  8.27 us (2%)
  other arithmetic  8.07 us (2%)
    psum x1, waiting for transfers between devices, on_device(): router_grad = lax.psum(router_term, ('dp', 'expert'))  123 us
    reduce_scatter x1, waiting for transfers between devices, on_device(): lax.psum_scatter(gate_up_part.astype(jnp.bfloat16), 'dp', scatter_dimensi...  49.5 us
    all_gather x1, waiting for transfers between devices, on_device(): lax.all_gather(down_weight, 'dp', axis=1, tiled=True)  46.4 us
    all_gather x1, waiting for transfers between devices, on_device(): lax.all_gather(gate_up_weight, 'dp', axis=1, tiled=True)  45.8 us
    all_to_all x1, waiting for transfers between devices, on_device(): lax.all_to_all(send_rows, 'expert', split_axis=0, concat_axis=0, tiled=True)  28.3 us
    all_to_all x1, waiting for transfers between devices, on_device(): lax.all_to_all(input_grad, 'expert', split_axis=0, concat_axis=0, tiled=T...  27.4 us
    all_to_all x1, waiting for transfers between devices, finish_rows(): lax.all_to_all(produced, 'expert', split_axis=0, concat_axis=0, tiled=True)  23.2 us
  transfers between devices with their start and end apart: 9, of which 7 were waited for; matrix products, arithmetic and copies ran while one was open for 10% of the time, Pallas kernels for 0%

commit v1 on v0

--- a/solution.py
+++ b/solution.py
@@ -96,7 +96,7 @@
     router_term = jnp.dot(
         tokens.astype(jnp.float32).T, logit_grads, precision=lax.Precision.HIGHEST
     )
-    router_grad = lax.psum(router_term, ("dp", "expert"))
+    router_grad = lax.psum(lax.psum(router_term, "expert"), "dp")
     gate_up_part = jnp.einsum(
         "sjcd,sjcf->jdf", received, pre_grad, preferred_element_type=jnp.float32
     )

time: 445 us -> 462 us (1.038)
  waiting for transfers between devices: 345 us -> 362 us
    psum x1 -> x2, waiting for transfers between devices: 123 us -> 40.2 us  [on_device(): router_grad = lax.psum(lax.psum(router_term, 'expert'), 'dp')]
    reduce_scatter x1, waiting for transfers between devices: 0.01 us -> 50.6 us  [on_device(): lax.psum_scatter(down_part.astype(jnp.bfloat16), 'dp', scatter_dimension=...]
    reduce_scatter x1, waiting for transfers between devices: 49.5 us -> 86.5 us  [on_device(): lax.psum_scatter(gate_up_part.astype(jnp.bfloat16), 'dp', scatter_dimensi...]
    all_to_all x1, waiting for transfers between devices: 23.2 us -> 31.3 us  [finish_rows(): lax.all_to_all(produced, 'expert', split_axis=0, concat_axis=0, tiled=True)]
  transfers between devices with their start and end apart: 9 -> 10, of which waited for: 7 -> 8; matrix products, arithmetic and copies ran while one was open for 10% -> 9% of each run, Pallas kernels for 0% -> 0%
where the time goes in v1:
time: 462 us; the launch traced here: 460 us
  waiting for transfers between devices  362 us (78%)
  matrix products  47.4 us (10%)
  starting transfers between devices  21.2 us (5%)
  between operations  14.3 us (3%)
  other arithmetic  8.07 us (2%)
  local copies, waits for them, and re-layouts  6.97 us (2%)
    reduce_scatter x1, waiting for transfers between devices, on_device(): lax.psum_scatter(gate_up_part.astype(jnp.bfloat16), 'dp', scatter_dimensi...  86.5 us
    reduce_scatter x1, waiting for transfers between devices, on_device(): lax.psum_scatter(down_part.astype(jnp.bfloat16), 'dp', scatter_dimension=...  50.6 us
    all_gather x1, waiting for transfers between devices, on_device(): lax.all_gather(down_weight, 'dp', axis=1, tiled=True)  46.4 us
    all_gather x1, waiting for transfers between devices, on_device(): lax.all_gather(gate_up_weight, 'dp', axis=1, tiled=True)  45.8 us
    psum x2, waiting for transfers between devices, on_device(): router_grad = lax.psum(lax.psum(router_term, 'expert'), 'dp')  40.2 us
    all_to_all x1, waiting for transfers between devices, on_device(): lax.all_to_all(input_grad, 'expert', split_axis=0, concat_axis=0, tiled=T...  31.7 us
    all_to_all x1, waiting for transfers between devices, finish_rows(): lax.all_to_all(produced, 'expert', split_axis=0, concat_axis=0, tiled=True)  31.3 us
    all_to_all x1, waiting for transfers between devices, on_device(): lax.all_to_all(send_rows, 'expert', split_axis=0, concat_axis=0, tiled=True)  28.2 us
  transfers between devices with their start and end apart: 10, of which 8 were waited for; matrix products, arithmetic and copies ran while one was open for 9% of the time, Pallas kernels for 0%

profile of v1, /device:TPU:1, one launch (start us, length us, event | category | flops | bytes accessed | tf_op | source)
XLA Modules:
  0.0 460.0 jit_solution(11968571833887685165)
XLA Ops:
  7.2 0.7 all-gather.3.cloned.1.call-update
  8.0 0.7 all-gather.5.cloned.1.call-update
  9.8 1.6 convolution_convert_fusion
  11.4 6.5 %all-to-all-start = ((bf16[8,2,40,1024]{3,2,1,0:T(8,128)(2,1)}), bf16[8,2,40,1024]{3,2,1,0:T(8,128)(2,1)S(1)}, u32[]{:S(2)}, u32[]{:S(2)}) async-start(bf16[8,2,40,1024]{3,2,1,0:T(8,128)(2,1)} %bitcast.3), calls=%async_computation | async-start | bytes 2621440 | tf_op jit(solution)/shard_map/all_to_all | solution.py:55
  18.8 2.0 bitcast_convert_fusion.2
  20.9 28.2 %all-to-all-done = bf16[8,2,40,1024]{3,2,1,0:T(8,128)(2,1)S(1)} async-done(((bf16[8,2,40,1024]{3,2,1,0:T(8,128)(2,1)}), bf16[8,2,40,1024]{3,2,1,0:T(8,128)(2,1)S(1)}, u32[]{:S(2)}, u32[]{:S(2)}) %all-to-all-start) | async-done | bytes 1310752 | tf_op jit(solution)/shard_map/all_to_all | solution.py:55
  49.1 4.4 all-to-all-start.2
  53.6 45.8 %all-gather.3.cloned.1.call-done = bf16[2,1024,2048]{2,1,0:T(8,128)(2,1)} async-done(((bf16[2,256,2048]{2,1,0:T(8,128)(2,1)}), bf16[2,1024,2048]{2,1,0:T(8,128)(2,1)}) %all-gather.3.cloned.1.call-update) | async-done | bytes 8388624 | tf_op jit(solution)/shard_map/all_gather | solution.py:25
  99.3 8.0 %fusion.8 = f32[8,2,40,2048]{3,2,0,1:T(8,128)} fusion(bf16[2,1024,2048]{2,1,0:T(8,128)(2,1)} %all-gather.3.cloned.1.call-done, bf16[8,2,40,1024]{3,2,1,0:T(8,128)(2,1)S(1)} %all-to-all-done), kind=kOutput, calls=%fused_computation.10 | convolution fusion | flops 2684354560 | bytes 14942208 | tf_op jit(solution)/shard_map/sjcd,jdf->sjcf/dot_general | solution.py:56
  107.4 46.4 %all-gather.5.cloned.1.call-done = bf16[2,1024,1024]{2,1,0:T(8,128)(2,1)} async-done(((bf16[2,256,1024]{2,1,0:T(8,128)(2,1)}), bf16[2,1024,1024]{2,1,0:T(8,128)(2,1)}) %all-gather.5.cloned.1.call-update) | async-done | bytes 4194320 | tf_op jit(solution)/shard_map/all_gather | solution.py:26
  153.8 8.2 %fusion.13 = (bf16[8,2,40,1024]{3,2,0,1:T(8,128)(2,1)}, bf16[8,2,40,1024]{3,2,0,1:T(8,128)(2,1)}, bf16[8,2,40,1024]{3,2,0,1:T(8,128)(2,1)S(1)}) fusion(f32[8,2,40,2048]{3,2,0,1:T(8,128)} %fusion.8, bf16[2,1024,1024]{2,1,0:T(8,128)(2,1)} %all-gather.5.cloned.1.call-done, bf16[8,2,40,1024]{3,2,1,0:T(8,128)(2,1)S(1)} %all-to-all-done.2), kind=kOutput, calls=%fused_computation.16 | convolution fusion | flops 1352007680 | bytes 14680064 | tf_op jit(solution)/shard_map/sjcd,jfd->sjcf/dot_general | solution.py:76
  162.0 1.5 fusion.26
  163.5 1.2 copy.38
  164.7 5.4 %all-to-all-start.1 = ((bf16[8,2,40,1024]{3,2,1,0:T(8,128)(2,1)}), bf16[8,2,40,1024]{3,2,1,0:T(8,128)(2,1)}, u32[]{:S(2)}, u32[]{:S(2)}) async-start(bf16[8,2,40,1024]{3,2,1,0:T(8,128)(2,1)} %copy.38), calls=%async_computation.1 | async-start | bytes 2621440 | tf_op jit(solution)/shard_map/all_to_all | solution.py:20
  170.2 31.3 %all-to-all-done.1 = bf16[8,2,40,1024]{3,2,1,0:T(8,128)(2,1)} async-done(((bf16[8,2,40,1024]{3,2,1,0:T(8,128)(2,1)}), bf16[8,2,40,1024]{3,2,1,0:T(8,128)(2,1)}, u32[]{:S(2)}, u32[]{:S(2)}) %all-to-all-start.1) | async-done | bytes 1310752 | tf_op jit(solution)/shard_map/all_to_all | solution.py:20
  201.5 3.1 multiply_reduce_fusion
  204.6 0.9 convolution_bitcast_fusion
  205.6 5.7 %bitcast_convert_fusion.1 = bf16[2,1024,1024]{2,1,0:T(8,128)(2,1)} fusion(bf16[8,2,40,1024]{3,2,0,1:T(8,128)(2,1)} %copy-done.8, bf16[8,2,40,1024]{3,2,1,0:T(8,128)(2,1)S(1)} %all-to-all-done.2), kind=kOutput, calls=%fused_computation.1 | convolution fusion | flops 1344274432 | bytes 6815744 | tf_op jit(solution)/shard_map/sjcf,sjcd->jfd/dot_general | solution.py:103
  211.5 1.1 copy-done.6
  212.6 8.1 %bitcast_convert_fusion = bf16[2,1024,2048]{2,1,0:T(8,128)(2,1)} fusion(bf16[8,2,40,1024]{3,2,1,0:T(8,128)(2,1)S(1)} %all-to-all-done, bf16[8,2,40,1024]{3,2,0,1:T(8,128)(2,1)} %get-tuple-element.10, bf16[8,2,40,1024]{3,2,0,1:T(8,128)(2,1)S(1)} %copy-done.6), kind=kOutput, calls=%fused_computation | convolution fusion | flops 2693791744 | bytes 12320768 | tf_op jit(solution)/shard_map/sjcd,sjcf->jdf/dot_general | solution.py:100
  220.7 1.3 copy-done.7
  222.0 6.3 %fusion.23 = bf16[8,2,40,1024]{3,2,0,1:T(8,128)(2,1)S(1)} fusion(bf16[2,1024,2048]{2,1,0:T(8,128)(2,1)} %all-gather.3.cloned.1.call-done, bf16[8,2,40,1024]{3,2,0,1:T(8,128)(2,1)S(1)} %copy-done.7, bf16[8,2,40,1024]{3,2,0,1:T(8,128)(2,1)S(1)} %copy-done.6), kind=kOutput, calls=%fused_computation.26 | convolution fusion | flops 2690252800 | bytes 12320768 | tf_op jit(solution)/shard_map/sjcf,jdf->sjcd/dot_general | solution.py:82
  228.3 1.2 copy.40
  229.5 4.4 all-to-all-start.3
  234.1 31.7 %all-to-all-done.3 = bf16[8,2,40,1024]{3,2,1,0:T(8,128)(2,1)S(1)} async-done(((bf16[8,2,40,1024]{3,2,1,0:T(8,128)(2,1)}), bf16[8,2,40,1024]{3,2,1,0:T(8,128)(2,1)S(1)}, u32[]{:S(2)}, u32[]{:S(2)}) %all-to-all-start.3) | async-done | bytes 1310752 | tf_op jit(solution)/shard_map/all_to_all | solution.py:85
  266.3 1.2 fusion.30
  267.5 50.6 %reduce-scatter.5.cloned.1.call-done = bf16[2,256,1024]{2,1,0:T(8,128)(2,1)} async-done(((bf16[2,1024,1024]{2,1,0:T(8,128)(2,1)}), bf16[2,256,1024]{2,1,0:T(8,128)(2,1)}) %reduce-scatter.5.cloned.1.call-update) | async-done | bytes 1048592 | tf_op jit(solution)/shard_map/reduce_scatter | solution.py:108
  318.1 2.8 convert_element_type.79
  320.9 86.5 %reduce-scatter.3.cloned.1.call-done = bf16[2,256,2048]{2,1,0:T(8,128)(2,1)} async-done(((bf16[2,1024,2048]{2,1,0:T(8,128)(2,1)}), bf16[2,256,2048]{2,1,0:T(8,128)(2,1)}) %reduce-scatter.3.cloned.1.call-update) | async-done | bytes 2097168 | tf_op jit(solution)/shard_map/reduce_scatter | solution.py:105
  407.4 4.1 convert_element_type.77
  411.5 40.2 %all-reduce.6.cloned.1.call-done = f32[1024,16]{0,1:T(8,128)} async-done(((f32[1024,16]{0,1:T(8,128)}), f32[1024,16]{0,1:T(8,128)}) %all-reduce.6.cloned.1.call-update) | async-done | bytes 65552 | tf_op jit(solution)/shard_map/psum | solution.py:99
  451.7 1.5 copy.62
  (48 shorter events, 3.0 us)
Async XLA Ops:
  7.2 2.6 copy-start
  7.2 1.5 copy-start.4
  7.2 92.2 %all-gather.3.cloned.1.call-start = ((), (), s32[]{:S(2)}) async-start(), calls=%async_computation.6 | async-start | bytes 10485760 | tf_op jit(solution)/shard_map/all_gather | solution.py:25
  7.9 145.9 %all-gather.5.cloned.1.call-start = ((), (), s32[]{:S(2)}) async-start(), calls=%async_computation.7 | async-start | bytes 5242880 | tf_op jit(solution)/shard_map/all_gather | solution.py:26
  11.4 6.5 %copy-start.2 = (bf16[160,1024]{1,0:T(8,128)(2,1)S(1)}, bf16[160,1024]{1,0:T(8,128)(2,1)}, u32[]{:S(2)}) copy-start(bf16[160,1024]{1,0:T(8,128)(2,1)} %param.11) | copy-start | bytes 983044
  11.4 6.6 %copy-start.3 = (bf16[1024,16]{0,1:T(8,128)(2,1)S(1)}, bf16[1024,16]{0,1:T(8,128)(2,1)}, u32[]{:S(2)}) copy-start(bf16[1024,16]{0,1:T(8,128)(2,1)} %param.8) | copy-start | bytes 98308
  11.4 37.7 %all-to-all-start = ((bf16[8,2,40,1024]{3,2,1,0:T(8,128)(2,1)}), bf16[8,2,40,1024]{3,2,1,0:T(8,128)(2,1)S(1)}, u32[]{:S(2)}, u32[]{:S(2)}) async-start(bf16[8,2,40,1024]{3,2,1,0:T(8,128)(2,1)} %bitcast.3), calls=%async_computation | async-start | bytes 2621440 | tf_op jit(solution)/shard_map/all_to_all | solution.py:55
  18.0 0.9 copy-start.1
  49.1 58.3 %all-to-all-start.2 = ((bf16[8,2,40,1024]{3,2,1,0:T(8,128)(2,1)}), bf16[8,2,40,1024]{3,2,1,0:T(8,128)(2,1)S(1)}, u32[]{:S(2)}, u32[]{:S(2)}) async-start(bf16[8,2,40,1024]{3,2,1,0:T(8,128)(2,1)} %bitcast.93), calls=%async_computation.2 | async-start | bytes 2621440 | tf_op jit(solution)/shard_map/all_to_all | solution.py:74
  153.8 8.2 %copy-start.5 = (bf16[2,1024,1024]{2,1,0:T(8,128)(2,1)S(1)}, bf16[2,1024,1024]{2,1,0:T(8,128)(2,1)}, u32[]{:S(2)}) copy-start(bf16[2,1024,1024]{2,1,0:T(8,128)(2,1)} %all-gather.5.cloned.1.call-done) | copy-start | bytes 12582916
  162.0 1.5 copy-start.8
  164.7 36.8 %all-to-all-start.1 = ((bf16[8,2,40,1024]{3,2,1,0:T(8,128)(2,1)}), bf16[8,2,40,1024]{3,2,1,0:T(8,128)(2,1)}, u32[]{:S(2)}, u32[]{:S(2)}) async-start(bf16[8,2,40,1024]{3,2,1,0:T(8,128)(2,1)} %copy.38), calls=%async_computation.1 | async-start | bytes 2621440 | tf_op jit(solution)/shard_map/all_to_all | solution.py:20
  170.1 96.1 %all-reduce.4.cloned.1.call-start = ((), (), s32[]{:S(2)}) async-start(), calls=%async_computation.8 | async-start | bytes 131072 | tf_op jit(solution)/shard_map/psum | solution.py:99
  205.5 112.6 %reduce-scatter.5.cloned.1.call-start = ((), (), s32[]{:S(2)}) async-start(), calls=%async_computation.11 | async-start | bytes 5242880 | tf_op jit(solution)/shard_map/reduce_scatter | solution.py:108
  211.3 1.3 copy-start.6
  211.3 196.1 %reduce-scatter.3.cloned.1.call-start = ((), (), s32[]{:S(2)}) async-start(), calls=%async_computation.10 | async-start | bytes 10485760 | tf_op jit(solution)/shard_map/reduce_scatter | solution.py:105
  220.7 1.3 copy-start.7
  229.5 36.3 %all-to-all-start.3 = ((bf16[8,2,40,1024]{3,2,1,0:T(8,128)(2,1)}), bf16[8,2,40,1024]{3,2,1,0:T(8,128)(2,1)S(1)}, u32[]{:S(2)}, u32[]{:S(2)}) async-start(bf16[8,2,40,1024]{3,2,1,0:T(8,128)(2,1)} %copy.40), calls=%async_computation.3 | async-start | bytes 2621440 | tf_op jit(solution)/shard_map/all_to_all | solution.py:85
  233.9 217.8 %all-reduce.6.cloned.1.call-start = ((), (), s32[]{:S(2)}) async-start(), calls=%async_computation.9 | async-start | bytes 131072 | tf_op jit(solution)/shard_map/psum | solution.py:99
Sparse Core Ops, SparseCore 0:
  9.8 89.4 all-gather.2
  101.2 52.5 all-gather.4
  205.6 54.3 all-reduce.3
  263.4 54.6 reduce-scatter.4
  321.0 86.3 reduce-scatter.2
  410.1 41.5 all-reduce.5
